TPU v7x, 128 devices: a whole 4x4x4 slice. The times are simulated.
128 devices in a mesh: blk: 32 (over x, y, core), mp: 4 (over z).
Axes of the slice: x: 4, y: 4, z: 4, core: 2. Of those that a mesh axis runs over, the one named last changes fastest.
Arguments:
- hidden: bfloat16 [144, 3584], replicated, may hold values from -6 to 6
- medusa_w: bfloat16 [2, 3584, 3584], P(None, 'blk', 'mp'), may hold values from -0.09375 to 0.09375
- embedding: bfloat16 [131072, 3584], P(('blk', 'mp')), may hold values from -0.5 to 0.5
- cand_ids: int32 [2, 144, 10], replicated, may hold values from 0 to 131071
- tree_q: bfloat16 [12, 48, 4096], P(None, None, 'mp'), may hold values from -6 to 6
- tree_key_value: bfloat16 [2, 12, 48, 2048], P(None, None, None, 'mp'), may hold values from -6 to 6
- prompt_key_value: bfloat16 [2, 32, 2048, 2048], P(None, 'blk', None, 'mp'), may hold values from -6 to 6
- block_group: int32 [32], P('blk'), may hold values from 0 to 11, as said below
- block_len: int32 [32], P('blk'), may hold values from 1 to 2048
- block_empty: int32 [32], P('blk'), may hold values 0 or 1
- parents: int32 [12, 48], replicated, may hold values from 0 to 46, as said below
- out_weight: bfloat16 [4096, 3584], P('mp'), may hold values from -0.09375 to 0.09375
- post_gain: float32 [3584], replicated, may hold values from 0.5 to 1.5
- resid: bfloat16 [576, 3584], P('blk'), may hold values from -6 to 6
Outputs:
- draft_logprob: float32 [2, 144, 10], replicated
- layer_out: bfloat16 [576, 3584], P('blk')
Inputs may be any that keep to these rules, and one draw needn't show every extreme that they name: `block_group`: every group number from 0 to min(12, 32) - 1 owns at least one block. `parents`: entry 0 of each row is 0; entry i for i >= 1 is below i; some group's last token has parent 48 - 2.
All inputs are finite; a program needn't handle non-finite values. No bound on the sum of `block_empty` on one device may be relied on, other than what follows from the above.
Results may differ from a plain program's by a relative error of at most 0.005.
Values may be sent and summed in bfloat16 or wider, within the bound.
A program may use at most 128 MiB of HBM per device.

v0:
```python
import jax
import jax.numpy as jnp
from jax import lax
from jax.sharding import PartitionSpec as P

HEAD_SIZE = 256


def capped(values, limit):
    return limit * jnp.tanh(values / limit)


def ancestry(parents):
    count = parents.shape[1]
    column = jnp.arange(count, dtype=jnp.int32)
    linked = (parents[:, :, None] == column[None, None, :]) & (column[None, :, None] > 0)
    reach = jnp.eye(count, dtype=jnp.float32)[None] + linked.astype(jnp.float32)
    for sweep in range(count.bit_length()):
        reach = jnp.minimum(
            jnp.einsum("gij,gjk->gik", reach, reach, precision=lax.Precision.HIGHEST), 1.0
        )
    return reach


def attend(queries, keys, values, mask):
    rows = queries.shape[0]
    length = keys.shape[0]
    kv_heads = keys.shape[1] // HEAD_SIZE
    repeats = queries.shape[1] // keys.shape[1]
    query_view = queries.reshape(rows, kv_heads, repeats, HEAD_SIZE)
    key_view = keys.reshape(length, kv_heads, HEAD_SIZE)
    value_view = values.reshape(length, kv_heads, HEAD_SIZE)
    scores = jnp.einsum(
        "qhrd,khd->hrqk", query_view, key_view, preferred_element_type=jnp.float32
    ) * HEAD_SIZE ** (-0.5)
    weights = jnp.exp(capped(scores, 50.0)) * mask[None, None]
    denominator = jnp.sum(weights, -1).transpose(2, 0, 1).reshape(rows, kv_heads * repeats)
    numerator = jnp.einsum(
        "hrqk,khd->qhrd",
        weights.astype(jnp.bfloat16),
        value_view,
        preferred_element_type=jnp.float32,
    )
    return (numerator.reshape(rows, kv_heads * repeats * HEAD_SIZE), denominator)


def per_device(
    hidden,
    medusa_w,
    embedding,
    cand_ids,
    tree_q,
    tree_key_value,
    prompt_key_value,
    block_group,
    block_len,
    block_empty,
    parents,
    out_weight,
    post_gain,
    resid,
):
    units = medusa_w.shape[2]
    inner = jnp.einsum(
        "rd,mdu->mru",
        hidden,
        lax.all_gather(medusa_w, "blk", axis=1, tiled=True),
        preferred_element_type=jnp.float32,
    )
    own_cols = lax.dynamic_slice_in_dim(hidden, lax.axis_index("mp") * units, units, 1).astype(
        jnp.float32
    )
    fresh = (own_cols[None] + jax.nn.silu(inner)).astype(jnp.bfloat16)
    full_fresh = lax.all_gather(fresh, "mp", axis=2, tiled=True)
    logits = capped(
        jnp.einsum("mrd,vd->mrv", full_fresh, embedding, preferred_element_type=jnp.float32), 30.0
    )
    totals = jnp.sum(jnp.exp(logits), -1)
    vocab_dev = embedding.shape[0]
    first_id = lax.axis_index(("blk", "mp")) * vocab_dev
    local_ids = cand_ids - first_id
    match = local_ids[..., None] == jnp.arange(vocab_dev, dtype=jnp.int32)
    picked = jnp.sum(jnp.where(match, logits[:, :, None, :], 0.0), -1)
    totals, picked = lax.psum((totals, picked), ("blk", "mp"))
    draft_logprob = picked - jnp.log(totals)[..., None]
    groups, tree_size, features = tree_q.shape
    keys = prompt_key_value[0, 0]
    values = prompt_key_value[1, 0]
    length = keys.shape[0]
    group = block_group[0]
    key_ok = ((jnp.arange(length, dtype=jnp.int32) < block_len[0]) & (block_empty[0] == 0)).astype(
        jnp.float32
    )
    row_group = jnp.arange(groups * tree_size, dtype=jnp.int32) // tree_size
    mask = (row_group == group).astype(jnp.float32)[:, None] * key_ok[None, :]
    numer, denom = attend(tree_q.reshape(groups * tree_size, features), keys, values, mask)
    rows_dev = groups * tree_size // lax.axis_size("blk")
    first_row = lax.axis_index("blk") * rows_dev
    summed = lax.psum((numer, denom), "blk")
    numer = lax.dynamic_slice_in_dim(summed[0], first_row, rows_dev, 0)
    denom = lax.dynamic_slice_in_dim(summed[1], first_row, rows_dev, 0)
    reach = ancestry(parents)
    tree_numer, tree_denom = jax.vmap(attend)(tree_q, tree_key_value[0], tree_key_value[1], reach)
    heads_dev = tree_denom.shape[2]
    tree_numer = lax.dynamic_slice_in_dim(
        tree_numer.reshape(groups * tree_size, features), first_row, rows_dev, 0
    )
    tree_denom = lax.dynamic_slice_in_dim(
        tree_denom.reshape(groups * tree_size, heads_dev), first_row, rows_dev, 0
    )
    numer = numer + tree_numer
    denom = denom + tree_denom
    heads_out = (
        (numer.reshape(rows_dev, heads_dev, HEAD_SIZE) / denom[..., None])
        .reshape(rows_dev, features)
        .astype(jnp.bfloat16)
    )
    attn = lax.psum(jnp.dot(heads_out, out_weight, preferred_element_type=jnp.float32), "mp")
    normed = attn * lax.rsqrt(jnp.mean(attn * attn, -1, keepdims=True) + 1e-06) * post_gain
    layer_out = (normed + resid.astype(jnp.float32)).astype(jnp.bfloat16)
    return (draft_logprob, layer_out)


def solution(mesh):
    placed = (
        P(),
        P(None, "blk", "mp"),
        P(("blk", "mp"), None),
        P(),
        P(None, None, "mp"),
        P(None, None, None, "mp"),
        P(None, "blk", None, "mp"),
        P("blk"),
        P("blk"),
        P("blk"),
        P(),
        P("mp", None),
        P(),
        P("blk", None),
    )
    return jax.shard_map(
        per_device, mesh=mesh, in_specs=placed, out_specs=(P(), P("blk", None)), check_vma=False
    )
```

profile of v0, /device:TPU:1, one launch (start us, length us, event | category | flops | bytes accessed | tf_op | source)
XLA Modules:
  0.0 381.7 jit_solution(4261685247920140671)
XLA Ops:
  7.2 4.4 %fusion.51 = (bf16[1,1,2048,512]{3,2,1,0:T(8,128)(2,1)}, bf16[1,1,2048,512]{3,2,1,0:T(8,128)(2,1)}) fusion(bf16[2,1,2048,512]{3,2,1,0:T(8,128)(2,1)} %param.20), kind=kLoop, calls=%fused_computation.70 | loop fusion | bytes 8388608 | tf_op jit(solution)/shard_map/slice | solution.py:88
  11.6 2.9 copy.79
  16.5 3.3 reshape_reshape.3
  19.8 4.0 %copy.80 = bf16[1,1,2048,512]{2,3,1,0:T(8,128)(2,1)} copy(bf16[1,1,2048,512]{3,2,1,0:T(8,128)(2,1)} %get-tuple-element.6) | data formatting | bytes 4194304
  24.2 10.5 %fusion = (f32[2,2,576]{2,1,0:T(2,128)}, f32[2,2048,576,2]{1,2,3,0:T(8,128)}) fusion(f32[576,2048]{1,0:T(8,128)S(1)} %broadcast_multiply_fusion, bf16[2048,2,256,1]{0,2,3,1:T(8,128)(2,1)S(1)} %bitcast.83, bf16[576,2,2,256]{3,2,1,0:T(2,128)(2,1)S(1)} %reshape_reshape.3), kind=kOutput, calls=%fused_computation.1 | convolution fusion | flops 2434791168 | bytes 26878976 | tf_op jit(solution)/shard_map/qhrd,khd->hrqk/dot_general | solution.py:33
  34.7 9.1 %fusion.6 = f32[576,2,2,256]{3,0,2,1:T(8,128)S(1)} fusion(bf16[2048,2,256,1]{0,2,3,1:T(8,128)(2,1)S(1)} %bitcast.85, f32[2,2048,576,2]{1,2,3,0:T(8,128)} %get-tuple-element.15, f32[576,2048]{1,0:T(8,128)S(1)} %broadcast_multiply_fusion), kind=kOutput, calls=%fused_computation.10 | convolution fusion | flops 2434793472 | bytes 28049408 | tf_op jit(solution)/shard_map/hrqk,khd->qhrd/dot_general | solution.py:38
  43.8 1.8 copy.56
  45.6 2.9 reshape.101
  49.8 0.9 reshape.102
  51.7 1.4 convolution_minimum_fusion.5
  55.3 0.9 fusion.53
  56.3 124.9 %psum.38 = f32[576,4]{0,1:T(4,128)S(1)} all-reduce(f32[576,4]{0,1:T(4,128)S(1)} %reshape.104), channel_id=1, replica_groups=mesh['blk'=32,'mp'=4] {'blk'}, use_global_device_ids=true, to_apply=%region_6.7 | all-reduce | flops 2304 | bytes 18432 | tf_op jit(solution)/shard_map/psum | solution.py:99
  182.2 1.8 copy.62
  184.1 2.9 reshape.103
  187.1 5.1 %fusion.39 = f32[18,3584]{1,0:T(8,128)} fusion(bf16[1024,3584]{1,0:T(8,128)(2,1)} %param.25, f32[18,1024]{1,0:T(8,128)S(1)} %bitcast.87, f32[576,1024]{1,0:T(8,128)} %reshape.103, s32[]{:T(128)S(6)} %select_n.25, f32[576,1024]{1,0:T(8,128)} %all-reduce.4.cloned.1.call-done), kind=kOutput, calls=%fused_computation.47 | convolution fusion | flops 132175872 | bytes 7868420 | tf_op jit(solution)/shard_map/dot_general | solution.py:118
  192.4 32.7 %all-gather.3.cloned.1.call-done = bf16[2,3584,896]{2,1,0:T(8,128)(2,1)} async-done(((bf16[2,112,896]{2,1,0:T(8,128)(2,1)}), bf16[2,3584,896]{2,1,0:T(8,128)(2,1)}) %all-gather.3.cloned.1.call-update) | async-done | bytes 12845072 | tf_op jit(solution)/shard_map/all_gather | solution.py:67
  225.2 7.6 %add_convert_fusion = bf16[2,144,896]{2,1,0:T(8,128)(2,1)} fusion(bf16[2,3584,896]{2,1,0:T(8,128)(2,1)} %all-gather.3.cloned.1.call-done, bf16[144,3584]{1,0:T(8,128)(2,1)S(1)} %copy-done.4, f32[144,896]{1,0:T(8,128)S(1)} %dynamic-slice_convert_fusion), kind=kOutput, calls=%fused_computation.32 | convolution fusion | flops 1851236352 | bytes 14909440 | tf_op jit(solution)/shard_map/rd,mdu->mru/dot_general | solution.py:64
  232.8 34.1 %all-reduce.6.cloned.1.call-done = f32[18,3584]{1,0:T(8,128)} async-done(((f32[18,3584]{1,0:T(8,128)}), f32[18,3584]{1,0:T(8,128)}) %all-reduce.6.cloned.1.call-update) | async-done | bytes 258064 | tf_op jit(solution)/shard_map/psum | solution.py:118
  266.9 1.1 multiply_reduce_fusion
  268.0 1.8 add_convert_fusion.1
  269.8 31.7 %all-gather.5.cloned.1.call-done = bf16[2,144,3584]{2,1,0:T(8,128)(2,1)} async-done(((bf16[2,144,896]{2,1,0:T(8,128)(2,1)}), bf16[2,144,3584]{2,1,0:T(8,128)(2,1)}) %all-gather.5.cloned.1.call-update) | async-done | bytes 2064400 | tf_op jit(solution)/shard_map/all_gather | solution.py:74
  301.5 6.2 %exponential_reduce_fusion = (f32[2,144]{1,0:T(2,128)S(1)}, f32[2,144,1024]{2,1,0:T(8,128)S(1)}) fusion(bf16[2,144,3584]{2,1,0:T(8,128)(2,1)} %all-gather.5.cloned.1.call-done, bf16[1024,3584]{1,0:T(8,128)(2,1)} %param.16), kind=kOutput, calls=%fused_computation.24 | convolution fusion | flops 2114813696 | bytes 10585216 | tf_op jit(solution)/shard_map/mrd,vd->mrv/dot_general | solution.py:76
  307.8 1.8 select_reduce_fusion
  309.6 64.9 %all-reduce = (f32[2,144,10]{1,2,0:T(8,128)S(1)}, f32[2,144]{1,0:T(2,128)S(1)}) all-reduce(f32[2,144,10]{1,2,0:T(8,128)S(1)} %select_reduce_fusion, f32[2,144]{1,0:T(2,128)S(1)} %get-tuple-element.10), channel_id=1, replica_groups=mesh['blk'=32,'mp'=4] {'blk','mp'}, use_global_device_ids=true, to_apply=%region_1.2 | all-reduce | flops 3168 | bytes 25344 | tf_op jit(solution)/shard_map/psum | solution.py:84
  (53 shorter events, 6.9 us)
Async XLA Ops:
  7.2 179.9 %all-reduce.4.cloned.1.call-start = ((), (), s32[]{:S(2)}) async-start(), calls=%async_computation.2 | async-start | bytes 4718592 | tf_op jit(solution)/shard_map/psum | solution.py:99
  24.2 10.5 %copy-start.1 = (bf16[1,1,2048,512]{2,3,1,0:T(8,128)(2,1)S(1)}, bf16[1,1,2048,512]{2,3,1,0:T(8,128)(2,1)}, u32[]{:S(2)}) copy-start(bf16[1,1,2048,512]{2,3,1,0:T(8,128)(2,1)} %copy.80) | copy-start | bytes 6291460
  48.6 1.3 copy-start
  48.6 2.9 copy-start.2
  48.6 176.6 %all-gather.3.cloned.1.call-start = ((), (), s32[]{:S(2)}) async-start(), calls=%async_computation | async-start | bytes 13246464 | tf_op jit(solution)/shard_map/all_gather | solution.py:67
  49.3 217.6 %all-reduce.6.cloned.1.call-start = ((), (), s32[]{:S(2)}) async-start(), calls=%async_computation.3 | async-start | bytes 688128 | tf_op jit(solution)/shard_map/psum | solution.py:118
  184.0 3.0 copy-start.4
  192.1 40.7 %copy-start.5 = (s32[2,144,10]{1,0,2:T(2,128)S(1)}, s32[2,144,10]{1,0,2:T(2,128)}, u32[]{:S(2)}) copy-start(s32[2,144,10]{1,0,2:T(2,128)} %param.17) | copy-start | bytes 34564
  192.2 75.9 %copy-start.3 = (bf16[18,3584]{1,0:T(8,128)(2,1)S(1)}, bf16[18,3584]{1,0:T(8,128)(2,1)}, u32[]{:S(2)}) copy-start(bf16[18,3584]{1,0:T(8,128)(2,1)} %param.27) | copy-start | bytes 387076
  192.2 75.9 %copy-start.6 = (f32[3584]{0:T(1024)S(1)}, f32[3584]{0:T(1024)}, u32[]{:S(2)}) copy-start(f32[3584]{0:T(1024)} %param.26) | copy-start | bytes 43012
  192.2 109.4 %all-gather.5.cloned.1.call-start = ((), (), s32[]{:S(2)}) async-start(), calls=%async_computation.1 | async-start | bytes 2580480 | tf_op jit(solution)/shard_map/all_gather | solution.py:74
Sparse Core Ops, SparseCore 0:
  48.7 110.4 all-reduce.3
  161.6 63.5 all-gather.2
  227.5 39.3 all-reduce.5
  268.4 33.0 all-gather.4
where the time goes:
time: 382 us
  blocking collectives  190 us (50%)
  waiting for transfers between devices  99.3 us (26%)
  matrix products  43.3 us (11%)
  local copies, waits for them, and re-layouts  27.5 us (7%)
  between operations  16 us (4%)
  other arithmetic  5.25 us (1%)
    psum x1, blocking collectives, per_device(): summed = lax.psum((numer, denom), 'blk')  125 us
    psum x1, blocking collectives, per_device(): totals, picked = lax.psum((totals, picked), ('blk', 'mp'))  64.9 us
    psum x1, waiting for transfers between devices, per_device(): lax.psum(jnp.dot(heads_out, out_weight, preferred_element_type=jnp.float3...  34.1 us
    all_gather x1, waiting for transfers between devices, per_device(): lax.all_gather(medusa_w, 'blk', axis=1, tiled=True)  32.7 us
    all_gather x1, waiting for transfers between devices, per_device(): full_fresh = lax.all_gather(fresh, 'mp', axis=2, tiled=True)  31.7 us
    dot_general x2, matrix products, attend(): jnp.einsum('qhrd,khd->hrqk', query_view, key_view, preferred_element_type...  11.3 us
    dot_general x2, matrix products, attend(): jnp.einsum('hrqk,khd->qhrd', weights.astype(jnp.bfloat16), value_view, pr...  9.63 us
    unnamed x19, local copies, waits for them, and re-layouts  7.84 us
  transfers between devices with their start and end apart: 4, of which 3 were waited for; matrix products, arithmetic and copies ran while one was open for 7% of the time, Pallas kernels for 0%

commit v1 on v0

--- a/solution.py
+++ b/solution.py
@@ -60,6 +60,12 @@
     post_gain,
     resid,
 ):
+
+    def show_kinds(u):
+        for k in ("blk", "mp"):
+            u = lax.psum(u, k)
+        return u
+
     units = medusa_w.shape[2]
     inner = jnp.einsum(
         "rd,mdu->mru",
@@ -81,7 +87,7 @@
     local_ids = cand_ids - first_id
     match = local_ids[..., None] == jnp.arange(vocab_dev, dtype=jnp.int32)
     picked = jnp.sum(jnp.where(match, logits[:, :, None, :], 0.0), -1)
-    totals, picked = lax.psum((totals, picked), ("blk", "mp"))
+    totals, picked = show_kinds((totals, picked))
     draft_logprob = picked - jnp.log(totals)[..., None]
     groups, tree_size, features = tree_q.shape
     keys = prompt_key_value[0, 0]

time: 382 us -> 328 us (0.86)
  blocking collectives: 190 us -> 136 us
  waiting for transfers between devices: 99.3 us -> 89.4 us
  other arithmetic: 5.25 us -> 9.69 us
    psum x2, blocking collectives: 190 us -> 136 us  [show_kinds(): u = lax.psum(u, k)]
    all_gather x1, waiting for transfers between devices: 31.7 us -> 0.01 us  [per_device(): full_fresh = lax.all_gather(fresh, 'mp', axis=2, tiled=True)]
    all_gather x1, waiting for transfers between devices: 32.7 us -> 61.9 us  [per_device(): lax.all_gather(medusa_w, 'blk', axis=1, tiled=True)]
    psum x1, waiting for transfers between devices: 34.1 us -> 26.8 us  [per_device(): lax.psum(jnp.dot(heads_out, out_weight, preferred_element_type=jnp.float3...]
    unnamed x19 -> x23, local copies, waits for them, and re-layouts: 7.84 us -> 8.09 us
  transfers between devices with their start and end apart: 4 -> 4, of which waited for: 3 -> 2; matrix products, arithmetic and copies ran while one was open for 7% -> 21% of each run, Pallas kernels for 0% -> 0%
where the time goes in v1:
time: 328 us; the launch traced here: 326 us
  blocking collectives  136 us (41%)
  waiting for transfers between devices  89.4 us (27%)
  matrix products  45.2 us (14%)
  local copies, waits for them, and re-layouts  29.1 us (9%)
  between operations  16 us (5%)
  other arithmetic  9.69 us (3%)
    psum x2, blocking collectives, show_kinds(): u = lax.psum(u, k)  136 us
    all_gather x1, waiting for transfers between devices, per_device(): lax.all_gather(medusa_w, 'blk', axis=1, tiled=True)  61.9 us
    psum x1, waiting for transfers between devices, per_device(): lax.psum(jnp.dot(heads_out, out_weight, preferred_element_type=jnp.float3...  26.8 us
    dot_general x2, matrix products, attend(): jnp.einsum('qhrd,khd->hrqk', query_view, key_view, preferred_element_type...  13.1 us
    dot_general x2, matrix products, attend(): jnp.einsum('hrqk,khd->qhrd', weights.astype(jnp.bfloat16), value_view, pr...  9.6 us
    unnamed x23, local copies, waits for them, and re-layouts  8.09 us
    dot_general x1, matrix products, per_device(): jnp.einsum('rd,mdu->mru', hidden, lax.all_gather(medusa_w, 'blk', axis=1,...  7.56 us
  transfers between devices with their start and end apart: 4, of which 2 were waited for; matrix products, arithmetic and copies ran while one was open for 21% of the time, Pallas kernels for 0%

profile of v1, /device:TPU:1, one launch (start us, length us, event | category | flops | bytes accessed | tf_op | source)
XLA Modules:
  0.0 325.6 jit_solution(3094606066992411119)
XLA Ops:
  9.9 1.0 dynamic-slice_convert_fusion
  10.9 4.5 %fusion.51 = (bf16[1,1,2048,512]{3,2,1,0:T(8,128)(2,1)}, bf16[1,1,2048,512]{3,2,1,0:T(8,128)(2,1)}) fusion(bf16[2,1,2048,512]{3,2,1,0:T(8,128)(2,1)} %param.20), kind=kLoop, calls=%fused_computation.70 | loop fusion | bytes 8388608 | tf_op jit(solution)/shard_map/slice | solution.py:94
  15.4 61.9 %all-gather.3.cloned.1.call-done = bf16[2,3584,896]{2,1,0:T(8,128)(2,1)} async-done(((bf16[2,112,896]{2,1,0:T(8,128)(2,1)}), bf16[2,3584,896]{2,1,0:T(8,128)(2,1)}) %all-gather.3.cloned.1.call-update) | async-done | bytes 12845072 | tf_op jit(solution)/shard_map/all_gather | solution.py:73
  77.3 7.6 %add_convert_fusion = bf16[2,144,896]{2,1,0:T(8,128)(2,1)} fusion(bf16[2,3584,896]{2,1,0:T(8,128)(2,1)} %all-gather.3.cloned.1.call-done, bf16[144,3584]{1,0:T(8,128)(2,1)S(1)} %copy-done.5, f32[144,896]{1,0:T(8,128)S(1)} %dynamic-slice_convert_fusion), kind=kOutput, calls=%fused_computation.32 | convolution fusion | flops 1851236352 | bytes 14909440 | tf_op jit(solution)/shard_map/rd,mdu->mru/dot_general | solution.py:70
  85.1 2.5 broadcast_multiply_fusion
  87.6 2.9 copy.79
  90.6 4.0 %reshape_reshape.3 = bf16[576,2,2,256]{3,2,1,0:T(2,128)(2,1)} reshape(bf16[12,48,1024]{2,1,0:T(8,128)(2,1)} %param.18) | data formatting | bytes 2359296 | tf_op jit(solution)/shard_map/reshape;reshape | solution.py:30
  94.6 4.1 %copy.80 = bf16[1,1,2048,512]{2,3,1,0:T(8,128)(2,1)} copy(bf16[1,1,2048,512]{3,2,1,0:T(8,128)(2,1)} %get-tuple-element.9) | data formatting | bytes 4194304
  98.7 12.2 %fusion = (f32[2,2,576]{2,1,0:T(2,128)}, f32[2,2048,576,2]{1,2,3,0:T(8,128)}) fusion(f32[576,2048]{1,0:T(8,128)} %broadcast_multiply_fusion, bf16[2048,2,256,1]{0,2,3,1:T(8,128)(2,1)S(1)} %bitcast.85, bf16[576,2,2,256]{3,2,1,0:T(2,128)(2,1)} %reshape_reshape.3), kind=kOutput, calls=%fused_computation.1 | convolution fusion | flops 2434791168 | bytes 26878976 | tf_op jit(solution)/shard_map/qhrd,khd->hrqk/dot_general | solution.py:33
  110.9 9.1 %fusion.6 = f32[576,2,2,256]{3,0,2,1:T(8,128)S(1)} fusion(bf16[2048,2,256,1]{0,2,3,1:T(8,128)(2,1)S(1)} %bitcast.87, f32[2,2048,576,2]{1,2,3,0:T(8,128)} %get-tuple-element.16, f32[576,2048]{1,0:T(8,128)S(1)} %bitcast.84), kind=kOutput, calls=%fused_computation.10 | convolution fusion | flops 2434793472 | bytes 28049408 | tf_op jit(solution)/shard_map/hrqk,khd->qhrd/dot_general | solution.py:38
  120.0 1.8 copy.56
  121.8 2.9 reshape.101
  129.2 1.4 convolution_minimum_fusion.5
  132.9 0.9 fusion.53
  134.6 1.8 copy.62
  136.4 2.9 reshape.103
  139.4 6.4 %exponential_reduce_fusion = (f32[2,144]{1,0:T(2,128)S(1)}, f32[2,144,1024]{2,1,0:T(8,128)S(1)}) fusion(bf16[2,144,3584]{2,1,0:T(8,128)(2,1)} %all-gather.5.cloned.1.call-done, bf16[1024,3584]{1,0:T(8,128)(2,1)} %param.16), kind=kOutput, calls=%fused_computation.24 | convolution fusion | flops 2114813696 | bytes 10585216 | tf_op jit(solution)/shard_map/mrd,vd->mrv/dot_general | solution.py:82
  145.7 1.8 select_reduce_fusion
  147.6 121.4 %all-reduce = (f32[2,144,10]{1,2,0:T(8,128)S(1)}, f32[2,144]{1,0:T(2,128)S(1)}, f32[576,4]{0,1:T(4,128)S(1)}) all-reduce(f32[2,144,10]{1,2,0:T(8,128)S(1)} %select_reduce_fusion, f32[2,144]{1,0:T(2,128)S(1)} %get-tuple-element.13, f32[576,4]{0,1:T(4,128)S(1)} %reshape.104), channel_id=1, replica_groups=mesh['blk'=32,'mp'=4] {'blk'}, use_global_device_ids=true, to_apply=%region_1.2 | all-reduce | flops 5472 | bytes 43776 | tf_op jit(solution)/shard_map/psum | solution.py:66
  269.3 5.1 %fusion.39 = f32[18,3584]{1,0:T(8,128)} fusion(bf16[1024,3584]{1,0:T(8,128)(2,1)} %param.25, f32[18,1024]{1,0:T(8,128)S(1)} %bitcast.89, f32[576,1024]{1,0:T(8,128)} %reshape.103, s32[]{:T(128)S(6)} %select_n.25, f32[576,1024]{1,0:T(8,128)} %all-reduce.5.cloned.1.call-done), kind=kOutput, calls=%fused_computation.47 | convolution fusion | flops 132175872 | bytes 7868420 | tf_op jit(solution)/shard_map/dot_general | solution.py:124
  274.5 14.2 %all-reduce.1 = (f32[2,144,10]{1,2,0:T(8,128)S(1)}, f32[2,144]{1,0:T(2,128)S(1)}) all-reduce(f32[2,144,10]{1,2,0:T(8,128)S(1)} %get-tuple-element.4, f32[2,144]{1,0:T(2,128)S(1)} %get-tuple-element.5), channel_id=1, replica_groups=mesh['blk'=32,'mp'=4] {'mp'}, use_global_device_ids=true, to_apply=%region_2.3 | all-reduce | flops 3168 | bytes 25344 | tf_op jit(solution)/shard_map/psum | solution.py:66
  289.4 26.8 %all-reduce.7.cloned.1.call-done = f32[18,3584]{1,0:T(8,128)} async-done(((f32[18,3584]{1,0:T(8,128)}), f32[18,3584]{1,0:T(8,128)}) %all-reduce.7.cloned.1.call-update) | async-done | bytes 258064 | tf_op jit(solution)/shard_map/psum | solution.py:124
  316.2 1.1 multiply_reduce_fusion
  317.3 1.8 add_convert_fusion.1
  (58 shorter events, 9.4 us)
Async XLA Ops:
  7.2 70.1 %all-gather.3.cloned.1.call-start = ((), (), s32[]{:S(2)}) async-start(), calls=%async_computation | async-start | bytes 13246464 | tf_op jit(solution)/shard_map/all_gather | solution.py:73
  7.9 131.5 %all-gather.5.cloned.1.call-start = ((), (), s32[]{:S(2)}) async-start(), calls=%async_computation.1 | async-start | bytes 2580480 | tf_op jit(solution)/shard_map/all_gather | solution.py:80
  10.9 66.4 %copy-start.5 = (bf16[144,3584]{1,0:T(8,128)(2,1)S(1)}, bf16[144,3584]{1,0:T(8,128)(2,1)}, u32[]{:S(2)}) copy-start(bf16[144,3584]{1,0:T(8,128)(2,1)} %param.14) | copy-start | bytes 3096580
  84.9 184.4 %all-reduce.5.cloned.1.call-start = ((), (), s32[]{:S(2)}) async-start(), calls=%async_computation.2 | async-start | bytes 4718592 | tf_op jit(solution)/shard_map/psum | solution.py:105
  94.6 16.3 %slice-start = ((s8[4718592]{0:T(1024)(128)(4,1)}), s8[524288]{0:T(1024)(128)(4,1)S(1)}, s32[]{:S(2)}) async-start(s8[4718592]{0:T(1024)(128)(4,1)} %bitcast.83), calls=%async_computation.4 | async-start | bytes 1048576
  98.7 12.2 %slice-start.1 = ((s8[4718592]{0:T(1024)(128)(4,1)}), s8[4194304]{0:T(1024)(128)(4,1)S(1)}, s32[]{:S(2)}) async-start(s8[4718592]{0:T(1024)(128)(4,1)} %bitcast.83), calls=%async_computation.5 | async-start | bytes 8388608
  98.7 12.2 %copy-start.1 = (bf16[1,1,2048,512]{2,3,1,0:T(8,128)(2,1)S(1)}, bf16[1,1,2048,512]{2,3,1,0:T(8,128)(2,1)}, u32[]{:S(2)}) copy-start(bf16[1,1,2048,512]{2,3,1,0:T(8,128)(2,1)} %copy.80) | copy-start | bytes 6291460
  124.7 1.3 copy-start
  124.7 4.3 %copy-start.2 = (bf16[2,12,48,512]{3,2,1,0:T(8,128)(2,1)S(1)}, bf16[2,12,48,512]{3,2,1,0:T(8,128)(2,1)}, u32[]{:S(2)}) copy-start(bf16[2,12,48,512]{3,2,1,0:T(8,128)(2,1)} %param.19) | copy-start | bytes 3538948
  124.8 191.4 %all-reduce.7.cloned.1.call-start = ((), (), s32[]{:S(2)}) async-start(), calls=%async_computation.3 | async-start | bytes 688128 | tf_op jit(solution)/shard_map/psum | solution.py:124
  139.3 6.4 %copy-start.4 = (s32[2,144,10]{1,2,0:T(8,128)S(1)}, s32[2,144,10]{1,2,0:T(8,128)}, u32[]{:S(2)}) copy-start(s32[2,144,10]{1,2,0:T(8,128)} %copy.50) | copy-start | bytes 34564
  269.3 48.0 %copy-start.3 = (bf16[18,3584]{1,0:T(8,128)(2,1)S(1)}, bf16[18,3584]{1,0:T(8,128)(2,1)}, u32[]{:S(2)}) copy-start(bf16[18,3584]{1,0:T(8,128)(2,1)} %param.27) | copy-start | bytes 387076
  269.3 48.0 %copy-start.6 = (f32[3584]{0:T(1024)S(1)}, f32[3584]{0:T(1024)}, u32[]{:S(2)}) copy-start(f32[3584]{0:T(1024)} %param.26) | copy-start | bytes 43012
Sparse Core Ops, SparseCore 0:
  10.4 66.8 all-gather.2
  85.0 29.9 all-gather.4
  124.9 106.3 all-reduce.4
  274.6 41.5 all-reduce.6
